TPU v7x, 32 devices: a whole 2x2x4 slice. The times are simulated.
32 devices in a mesh: band: 4 (over y, core), ga: 8 (over z, x).
Axes of the slice: x: 2, y: 2, z: 4, core: 2. Of those that a mesh axis runs over, the one named last changes fastest.
Arguments:
- density: float32 [160, 160, 160], P('ga'), may hold values from -6 to 6
- stick_column: int32 [20480], replicated, may hold values from 0 to 25599, as said below
- vloc: float32 [2, 160, 20480], P(None, None, 'ga'), may hold values from -0.0034179688 to 0.0034179688
- positions: float32 [3, 32], replicated, may hold values from 0 to 1
- species: int32 [32], replicated, may hold values from 0 to 1
- psi: bfloat16 [270336, 2, 1024], P('ga', None, 'band'), may hold values from -6 to 6
- miller_wave: int32 [3, 270336], P(None, 'ga'), may hold values from -40 to 40
- proj_radial: float32 [2, 8, 270336], P(None, None, 'ga'), may hold values from -0.01171875 to 0.01171875
- proj_count: int32 [2], replicated, may hold values from 4 to 8
- dcoef: float32 [2, 8, 8], replicated, may hold values from -0.0625 to 0.0625
- occupation: float32 [1024], P('band'), may hold values from 0 to 2
Outputs:
- density_sticks: float32 [2, 160, 20480], P(None, None, 'ga')
- forces: float32 [3, 32], replicated
Inputs may be any that keep to these rules, and one draw needn't show every extreme that they name: `stick_column`: distinct columns of the 160 by 160 frequency plane.
All inputs are finite; a program needn't handle non-finite values.
Results may differ from a plain program's by a relative error of at most 0.0036.
Values sent between devices are 32-bit elements; how exact they have to be, the bound alone decides.
A program may use at most 192 MiB of HBM per device.

v0:
```python
import math
import jax
import jax.numpy as jnp
from jax import lax
from jax.sharding import PartitionSpec as P

NX = 160
NY = 160
NZ = 160
TWO_PI = 2.0 * math.pi
EXACT = lax.Precision.HIGHEST
FINE = lax.Precision.HIGH


def frequency(index, count):
    return jnp.where(index >= count // 2, index - count, index)


def dft_table(count):
    index = jnp.arange(count, dtype=jnp.int32)
    angle = TWO_PI / count * (index[:, None] * index[None, :] % count).astype(jnp.float32)
    return (jnp.cos(angle), jnp.sin(angle))


def shards(
    density,
    stick_column,
    vloc,
    positions,
    species,
    psi,
    miller_wave,
    proj_radial,
    proj_count,
    dcoef,
    occupation,
):
    ga_index = lax.axis_index("ga")
    band_index = lax.axis_index("band")
    ga_count = lax.axis_size("ga")
    band_count = lax.axis_size("band")
    atom_count = positions.shape[1]
    kind_count = vloc.shape[0]
    slot_count = proj_radial.shape[1]
    sticks_here = vloc.shape[2]
    planes = density.shape[0]
    scale_norm = 1.0 / math.sqrt(NX * NY * NZ)
    start_zero = jnp.int32(0)
    cos_y, sin_y = dft_table(NY)
    cos_x, sin_x = dft_table(NX)
    batch_cos = jnp.broadcast_to(cos_x[None], (planes, NX, NX))
    batch_sin = jnp.broadcast_to(sin_x[None], (planes, NX, NX))
    xpass_real = jnp.einsum("pmx,pxy->pmy", batch_cos, density, precision=FINE).reshape(
        planes * NX, NY
    )
    xpass_imag = -jnp.einsum("pmx,pxy->pmy", batch_sin, density, precision=FINE).reshape(
        planes * NX, NY
    )
    full_real = jnp.dot(xpass_real, cos_y, precision=FINE) + jnp.dot(
        xpass_imag, sin_y, precision=FINE
    )
    full_imag = jnp.dot(xpass_imag, cos_y, precision=FINE) - jnp.dot(
        xpass_real, sin_y, precision=FINE
    )
    columns = jnp.concatenate(
        [full_real.reshape(planes, NX * NY), full_imag.reshape(planes, NX * NY)], axis=0
    )
    sub_sticks = sticks_here // band_count
    share_columns = lax.dynamic_slice_in_dim(
        stick_column.reshape(ga_count, band_count, sub_sticks), band_index, 1, 1
    ).reshape(ga_count * sub_sticks)
    picked_rows = jnp.take(columns.T, share_columns, axis=0)
    chosen = picked_rows.T.reshape(2 * planes, ga_count, sub_sticks).transpose(1, 0, 2)
    by_stick = lax.all_to_all(chosen, "ga", split_axis=0, concat_axis=0, tiled=True)
    by_stick = by_stick.reshape(ga_count * 2 * planes, sub_sticks)
    cos_z, sin_z = dft_table(NZ)
    cos_z = cos_z.reshape(NZ, ga_count, planes) * scale_norm
    sin_z = sin_z.reshape(NZ, ga_count, planes) * scale_norm
    table_z = jnp.stack(
        [jnp.stack([cos_z, sin_z], axis=2), jnp.stack([-sin_z, cos_z], axis=2)]
    ).reshape(2 * NZ, ga_count * 2 * planes)
    sub_values = jnp.dot(table_z, by_stick, precision=FINE).reshape(2, NZ, sub_sticks)
    density_sticks = lax.all_gather(sub_values, "band", axis=2, tiled=True)
    stick_start = ga_index * sticks_here + band_index * sub_sticks
    owned = lax.dynamic_slice_in_dim(stick_column, stick_start, sub_sticks)
    freq_x = frequency(owned // NY, NX).astype(jnp.float32)
    freq_y = frequency(owned % NY, NY).astype(jnp.float32)
    freq_z = frequency(jnp.arange(NZ, dtype=jnp.int32), NZ).astype(jnp.float32)
    wave_x = TWO_PI / NX * freq_x
    wave_y = TWO_PI / NY * freq_y
    wave_z = TWO_PI / NZ * freq_z
    angle_plane = TWO_PI * (
        positions[0][:, None] * freq_x[None, :] + positions[1][:, None] * freq_y[None, :]
    )
    angle_depth = TWO_PI * positions[2][:, None] * freq_z[None, :]
    plane_cos = jnp.cos(angle_plane)
    plane_sin = jnp.sin(angle_plane)
    plane_rows = jnp.stack(
        [
            plane_cos * wave_x[None, :],
            plane_cos * wave_y[None, :],
            plane_cos,
            plane_sin * wave_x[None, :],
            plane_sin * wave_y[None, :],
            plane_sin,
        ]
    ).reshape(6 * atom_count, sub_sticks)
    vloc_here = lax.dynamic_slice_in_dim(vloc, band_index * sub_sticks, sub_sticks, 2)
    fields = (vloc_here[:, None] * sub_values[None]).reshape(kind_count * 2 * NZ, sub_sticks)
    sums = lax.dot_general(plane_rows, fields, (((1,), (1,)), ((), ())), precision=FINE)
    sums = sums.reshape(2, 3, atom_count, kind_count, 2, NZ)
    all_pick = (species[:, None] == jnp.arange(kind_count, dtype=jnp.int32)[None, :]).astype(
        jnp.float32
    )
    sums = jnp.sum(sums * all_pick[None, None, :, :, None, None], axis=3)
    summed_real = sums[0, :, :, 0] - sums[1, :, :, 1]
    summed_imag = sums[0, :, :, 1] + sums[1, :, :, 0]
    depth_weight = jnp.stack([jnp.ones_like(wave_z), jnp.ones_like(wave_z), wave_z])
    local_part = jnp.sum(
        (jnp.cos(angle_depth)[None] * summed_imag + jnp.sin(angle_depth)[None] * summed_real)
        * depth_weight[:, None, :],
        axis=2,
    )
    bands_here = psi.shape[2]
    waves_here = psi.shape[0]
    psi_flat = psi.reshape(waves_here, 2 * bands_here)
    miller_f = miller_wave.astype(jnp.float32)
    weights = jnp.stack(
        [
            jnp.ones_like(miller_f[0]),
            TWO_PI / NX * miller_f[0],
            TWO_PI / NY * miller_f[1],
            TWO_PI / NZ * miller_f[2],
        ]
    )

    def project_block(block_start, block_rows):
        block_atoms = block_rows // slot_count
        atom_start = block_start // slot_count
        block_places = lax.dynamic_slice_in_dim(positions, atom_start, block_atoms, 1)
        block_kinds = lax.dynamic_slice_in_dim(species, atom_start, block_atoms)
        phase = TWO_PI * (
            block_places[0][:, None] * miller_f[0][None, :]
            + block_places[1][:, None] * miller_f[1][None, :]
            + block_places[2][:, None] * miller_f[2][None, :]
        )
        radial = jnp.zeros((block_atoms, slot_count, waves_here), jnp.float32)
        for kind_index in range(kind_count):
            match = (block_kinds == kind_index).astype(jnp.float32)
            radial = radial + match[:, None, None] * proj_radial[kind_index][None]
        parts = jnp.stack(
            [radial * jnp.cos(phase)[:, None, :], radial * jnp.sin(phase)[:, None, :]], axis=2
        )
        table = (parts[:, :, None] * weights[None, None, :, None, :]).astype(jnp.bfloat16)
        product = jnp.dot(
            table.reshape(block_rows * 8, waves_here), psi_flat, preferred_element_type=jnp.float32
        )
        product = product.reshape(block_rows, 4, 2, 2, bands_here)
        proj_real = product[:, :, 0, 0] - product[:, :, 1, 1]
        proj_imag = product[:, :, 0, 1] + product[:, :, 1, 0]
        return jnp.stack([proj_real, proj_imag], axis=2).reshape(block_rows, 8 * bands_here)

    share_rows = atom_count * slot_count // ga_count
    block_rows = 64
    starts = block_rows * jnp.arange(
        share_rows * lax.axis_size("ga") // block_rows, dtype=jnp.int32
    )

    def one_block(block_start):
        return project_block(block_start, block_rows)

    owned_rows = lax.psum_scatter(
        lax.map(one_block, starts).reshape(share_rows * lax.axis_size("ga"), 8 * bands_here),
        "ga",
        scatter_dimension=0,
        tiled=True,
    )
    per_ga = share_rows // slot_count
    ga_start = ga_index * per_ga
    terms = owned_rows.reshape(per_ga, slot_count, 4, 2, bands_here)
    ga_kinds = lax.dynamic_slice_in_dim(species, ga_start, per_ga)
    ga_pick = (ga_kinds[:, None] == jnp.arange(kind_count, dtype=jnp.int32)[None, :]).astype(
        jnp.float32
    )
    live_slots = (jnp.arange(slot_count, dtype=jnp.int32)[None, :] < proj_count[:, None]).astype(
        jnp.float32
    )
    kind_table = dcoef * live_slots[:, :, None] * live_slots[:, None, :]
    coupling = jnp.einsum("as,sij->aij", ga_pick, kind_table, precision=EXACT)
    mixed_real = jnp.einsum("aij,ajcn->aicn", coupling, terms[:, :, 1:, 0], precision=EXACT)
    mixed_imag = jnp.einsum("aij,ajcn->aicn", coupling, terms[:, :, 1:, 1], precision=EXACT)
    value = (
        terms[:, :, 0, 0][:, :, None, :] * mixed_imag
        - terms[:, :, 0, 1][:, :, None, :] * mixed_real
    )
    nonlocal_part = 2.0 * jnp.einsum("aicn,n->ca", value, occupation, precision=EXACT)
    nonlocal_full = lax.dynamic_update_slice(
        jnp.zeros((3, atom_count), jnp.float32), nonlocal_part, (start_zero, ga_start)
    )
    forces = lax.psum(local_part + nonlocal_full, ("band", "ga"))
    return (density_sticks, forces)


def solution(mesh):
    in_specs = (
        P("ga", None, None),
        P(),
        P(None, None, "ga"),
        P(),
        P(),
        P("ga", None, "band"),
        P(None, "ga"),
        P(None, None, "ga"),
        P(),
        P(),
        P("band"),
    )
    out_specs = (P(None, None, "ga"), P())
    return jax.shard_map(shards, mesh=mesh, in_specs=in_specs, out_specs=out_specs, check_vma=False)
```

profile of v0, /device:TPU:12, one launch (start us, length us, event | category | flops | bytes accessed | tf_op | source)
XLA Modules:
  0.0 485.3 jit_solution(1100664189729486365)
XLA Ops:
  8.6 1.4 convert_element_type.119
  12.0 83.8 %copy.56 = bf16[33792,2,256]{0,2,1:T(8,128)(2,1)} copy(bf16[33792,2,256]{2,1,0:T(2,128)(2,1)} %param.18) | data formatting | bytes 69206016 | tf_op args[5]
  95.8 2.2 pad_maximum_fusion.3
  98.0 206.9 %while.12 = (s32[]{:T(128)}, f32[4,64,2048]{2,1,0:T(8,128)}, s32[4]{0:T(128)}, s32[32]{0:T(128)S(1)}, f32[2,8,33792]{2,1,0:T(8,128)}, /*index=5*/f32[3,32]{1,0:T...) while((s32[]{:T(128)}, f32[4,64,2048]{2,1,0:T(8,128)}, ...), condition=%wide.region_3.4_spmd, body=%wide.region_2.3_spmd.sunk | while | flops 17768366080 | bytes 134012464 | solution.py:173
  98.0 1.2 dynamic_slice.49
  101.9 1.9 fusion.114
  103.8 5.2 %fusion.115 = (f32[8,33792]{1,0:T(8,128)}, f32[8,33792]{1,0:T(8,128)}) fusion(f32[33792]{0:T(1024)S(1)} %bitcast.204, f32[8]{0:T(128)S(1)} %get-tuple-element.244, f32[33792]{0:T(1024)S(1)} %bitcast.205, f32[8]{0:T(128)S(1)} %get-tuple-element.246, f32[33792]{0:T(1024)S(1)} %bitcast.203, f32[8]{0:T(128)S(1)} %get-tuple-element.248), kind=kLoop, calls=%fused_computation.14.clone.1 | loop fusion | flops 1622016 | bytes 2568288 | tf_op jit(solution)/shard_map/while/body/eval_jaxpr/cos | solution.py:152
  109.4 1.9 slice_bitcast_fusion.14
  111.6 2.2 bitcast_multiply_fusion.6
  113.8 6.2 %pad_maximum_fusion.8 = f32[64,2,33792]{2,0,1:T(8,128)} fusion(f32[64,1,33792]{2,0,1:T(8,128)S(1)} %get-tuple-element.255, f32[64,1,33792]{2,0,1:T(8,128)S(1)} %get-tuple-element.256), kind=kLoop, calls=%fused_computation.6.clone.1 | loop fusion | flops 4325376 | bytes 34603008 | tf_op jit(solution)/shard_map/while/body/eval_jaxpr/stack | solution.py:151
  120.0 24.2 %fusion.116 = f32[64,4,2,2,256]{4,0,3,2,1:T(8,128)S(1)} fusion(bf16[2,256,33792,1,1]{2,1,0,4,3:T(8,128)(2,1)} %bitcast.198, f32[4,33792]{1,0:T(4,128)S(1)} %copy-done.5, f32[64,2,33792]{2,0,1:T(8,128)} %pad_maximum_fusion.8), kind=kOutput, calls=%fused_computation.3.clone.1 | convolution fusion | flops 17751343104 | bytes 53493760 | tf_op jit(solution)/shard_map/while/body/eval_jaxpr/dot_general | solution.py:155
  145.5 2.3 broadcast_in_dim.34
  147.8 1.9 constant_dynamic-update-slice_fusion.2
  153.6 1.9 fusion.114
  155.5 5.2 %fusion.115 = (f32[8,33792]{1,0:T(8,128)}, f32[8,33792]{1,0:T(8,128)}) fusion(f32[33792]{0:T(1024)S(1)} %bitcast.204, f32[8]{0:T(128)S(1)} %get-tuple-element.244, f32[33792]{0:T(1024)S(1)} %bitcast.205, f32[8]{0:T(128)S(1)} %get-tuple-element.246, f32[33792]{0:T(1024)S(1)} %bitcast.203, f32[8]{0:T(128)S(1)} %get-tuple-element.248), kind=kLoop, calls=%fused_computation.14.clone.1 | loop fusion | flops 1622016 | bytes 2568288 | tf_op jit(solution)/shard_map/while/body/eval_jaxpr/cos | solution.py:152
  161.1 1.9 slice_bitcast_fusion.14
  163.3 2.2 bitcast_multiply_fusion.6
  165.5 6.2 %pad_maximum_fusion.8 = f32[64,2,33792]{2,0,1:T(8,128)} fusion(f32[64,1,33792]{2,0,1:T(8,128)S(1)} %get-tuple-element.255, f32[64,1,33792]{2,0,1:T(8,128)S(1)} %get-tuple-element.256), kind=kLoop, calls=%fused_computation.6.clone.1 | loop fusion | flops 4325376 | bytes 34603008 | tf_op jit(solution)/shard_map/while/body/eval_jaxpr/stack | solution.py:151
  171.7 24.2 %fusion.116 = f32[64,4,2,2,256]{4,0,3,2,1:T(8,128)S(1)} fusion(bf16[2,256,33792,1,1]{2,1,0,4,3:T(8,128)(2,1)} %bitcast.198, f32[4,33792]{1,0:T(4,128)S(1)} %copy-done.5, f32[64,2,33792]{2,0,1:T(8,128)} %pad_maximum_fusion.8), kind=kOutput, calls=%fused_computation.3.clone.1 | convolution fusion | flops 17751343104 | bytes 53493760 | tf_op jit(solution)/shard_map/while/body/eval_jaxpr/dot_general | solution.py:155
  197.2 2.3 broadcast_in_dim.34
  199.5 1.9 constant_dynamic-update-slice_fusion.2
  205.3 1.9 fusion.114
  207.2 5.2 %fusion.115 = (f32[8,33792]{1,0:T(8,128)}, f32[8,33792]{1,0:T(8,128)}) fusion(f32[33792]{0:T(1024)S(1)} %bitcast.204, f32[8]{0:T(128)S(1)} %get-tuple-element.244, f32[33792]{0:T(1024)S(1)} %bitcast.205, f32[8]{0:T(128)S(1)} %get-tuple-element.246, f32[33792]{0:T(1024)S(1)} %bitcast.203, f32[8]{0:T(128)S(1)} %get-tuple-element.248), kind=kLoop, calls=%fused_computation.14.clone.1 | loop fusion | flops 1622016 | bytes 2568288 | tf_op jit(solution)/shard_map/while/body/eval_jaxpr/cos | solution.py:152
  212.8 1.9 slice_bitcast_fusion.14
  215.1 2.2 bitcast_multiply_fusion.6
  217.3 6.2 %pad_maximum_fusion.8 = f32[64,2,33792]{2,0,1:T(8,128)} fusion(f32[64,1,33792]{2,0,1:T(8,128)S(1)} %get-tuple-element.255, f32[64,1,33792]{2,0,1:T(8,128)S(1)} %get-tuple-element.256), kind=kLoop, calls=%fused_computation.6.clone.1 | loop fusion | flops 4325376 | bytes 34603008 | tf_op jit(solution)/shard_map/while/body/eval_jaxpr/stack | solution.py:151
  223.4 24.2 %fusion.116 = f32[64,4,2,2,256]{4,0,3,2,1:T(8,128)S(1)} fusion(bf16[2,256,33792,1,1]{2,1,0,4,3:T(8,128)(2,1)} %bitcast.198, f32[4,33792]{1,0:T(4,128)S(1)} %copy-done.5, f32[64,2,33792]{2,0,1:T(8,128)} %pad_maximum_fusion.8), kind=kOutput, calls=%fused_computation.3.clone.1 | convolution fusion | flops 17751343104 | bytes 53493760 | tf_op jit(solution)/shard_map/while/body/eval_jaxpr/dot_general | solution.py:155
  249.0 2.3 broadcast_in_dim.34
  251.2 1.9 constant_dynamic-update-slice_fusion.2
  257.0 1.9 fusion.114
  258.9 5.2 %fusion.115 = (f32[8,33792]{1,0:T(8,128)}, f32[8,33792]{1,0:T(8,128)}) fusion(f32[33792]{0:T(1024)S(1)} %bitcast.204, f32[8]{0:T(128)S(1)} %get-tuple-element.244, f32[33792]{0:T(1024)S(1)} %bitcast.205, f32[8]{0:T(128)S(1)} %get-tuple-element.246, f32[33792]{0:T(1024)S(1)} %bitcast.203, f32[8]{0:T(128)S(1)} %get-tuple-element.248), kind=kLoop, calls=%fused_computation.14.clone.1 | loop fusion | flops 1622016 | bytes 2568288 | tf_op jit(solution)/shard_map/while/body/eval_jaxpr/cos | solution.py:152
  264.6 1.9 slice_bitcast_fusion.14
  266.8 2.2 bitcast_multiply_fusion.6
  269.0 6.2 %pad_maximum_fusion.8 = f32[64,2,33792]{2,0,1:T(8,128)} fusion(f32[64,1,33792]{2,0,1:T(8,128)S(1)} %get-tuple-element.255, f32[64,1,33792]{2,0,1:T(8,128)S(1)} %get-tuple-element.256), kind=kLoop, calls=%fused_computation.6.clone.1 | loop fusion | flops 4325376 | bytes 34603008 | tf_op jit(solution)/shard_map/while/body/eval_jaxpr/stack | solution.py:151
  275.1 24.2 %fusion.116 = f32[64,4,2,2,256]{4,0,3,2,1:T(8,128)S(1)} fusion(bf16[2,256,33792,1,1]{2,1,0,4,3:T(8,128)(2,1)} %bitcast.198, f32[4,33792]{1,0:T(4,128)S(1)} %copy-done.5, f32[64,2,33792]{2,0,1:T(8,128)} %pad_maximum_fusion.8), kind=kOutput, calls=%fused_computation.3.clone.1 | convolution fusion | flops 17751343104 | bytes 53493760 | tf_op jit(solution)/shard_map/while/body/eval_jaxpr/dot_general | solution.py:155
  300.7 2.3 broadcast_in_dim.34
  302.9 1.9 constant_dynamic-update-slice_fusion.2
  304.9 1.3 fusion.41
  307.7 2.5 fusion.15
  310.3 2.2 fusion.57
  312.5 1.6 convolution_negate_fusion
  314.1 3.5 fusion.55
  317.6 3.6 convolution_add_fusion
  321.2 3.4 copy.50
  324.7 5.5 %reshape.1345 = f32[20,25600]{1,0:T(8,128)} reshape(f32[3200,160]{1,0:T(8,128)} %copy.50) | data formatting | bytes 4096000 | tf_op jit(solution)/shard_map/reshape | solution.py:66
  330.2 6.1 %convolution_subtract_fusion = f32[3200,160]{0,1:T(8,128)} fusion(f32[3200,160]{0,1:T(8,128)} %fusion.55, f32[3200,160]{1,0:T(8,128)} %bitcast.200), kind=kOutput, calls=%fused_computation.31 | convolution fusion | flops 492262400 | bytes 6144000 | tf_op jit(solution)/shard_map/dot_general | solution.py:62
  336.3 3.4 copy.51
  339.7 5.4 %reshape.1346 = f32[20,25600]{1,0:T(8,128)} reshape(f32[3200,160]{1,0:T(8,128)} %copy.51) | data formatting | bytes 4096000 | tf_op jit(solution)/shard_map/reshape | solution.py:66
  345.1 4.7 pad_maximum_fusion.2
  349.9 9.0 %copy.52 = f32[40,25600]{0,1:T(8,128)} copy(f32[40,25600]{1,0:T(8,128)} %pad_maximum_fusion.2) | data formatting | bytes 8192000 | tf_op jit(solution)/shard_map/concatenate | solution.py:65
  358.9 22.7 %gather_fusion = f32[5120,40]{1,0:T(8,128)} fusion(f32[25600,40]{1,0:T(8,128)} %bitcast.196, s32[5120]{0:T(1024)S(1)} %broadcast_clamp_fusion), kind=kCustom, calls=%fused_computation | custom fusion | bytes 1658880 | tf_op jit(solution)/shard_map/jit(_take)/gather | solution.py:72
  381.7 5.3 %broadcast_select_fusion = f32[5120,40]{1,0:T(8,128)} fusion(f32[5120,40]{1,0:T(8,128)} %gather_fusion, pred[5120]{0:T(1024)(128)(4,1)S(1)} %compare_and_fusion), kind=kLoop, calls=%fused_computation.41 | loop fusion | flops 204800 | bytes 1643520 | tf_op jit(solution)/shard_map/jit(_take)/select_n | solution.py:72
  386.9 2.8 copy.53
  389.8 6.3 %all-to-all-start = ((f32[8,40,640]{2,1,0:T(8,128)}), f32[8,40,640]{2,1,0:T(8,128)}, u32[]{:S(2)}, u32[]{:S(2)}) async-start(f32[8,40,640]{2,1,0:T(8,128)} %bitcast.207), calls=%async_computation | async-start | bytes 1638400 | tf_op jit(solution)/shard_map/all_to_all | solution.py:74
  397.9 1.7 stack.25
  400.8 1.8 stack.27
  402.6 1.8 copy.49
  404.4 10.9 %all-to-all-done = f32[8,40,640]{2,1,0:T(8,128)} async-done(((f32[8,40,640]{2,1,0:T(8,128)}), f32[8,40,640]{2,1,0:T(8,128)}, u32[]{:S(2)}, u32[]{:S(2)}) %all-to-all-start) | async-done | bytes 819232 | tf_op jit(solution)/shard_map/all_to_all | solution.py:74
  415.2 3.0 fusion.27
  423.8 2.4 fusion.20
  426.9 1.2 reshape.1352
  430.8 1.4 add.270
  432.1 41.9 %psum.7 = f32[3,32]{1,0:T(4,128)} all-reduce(f32[3,32]{1,0:T(4,128)} %add.270), channel_id=1, replica_groups=mesh['band'=4,'ga'=8] {'band','ga'}, use_global_device_ids=true, to_apply=%region_6.7 | all-reduce | flops 96 | bytes 768 | tf_op jit(solution)/shard_map/psum | solution.py:200
  474.0 3.9 copy.109
  (134 shorter events, 28.0 us)
Async XLA Ops:
  8.0 299.7 %copy-start = (f32[20,160,160]{2,1,0:T(8,128)S(1)}, f32[20,160,160]{2,1,0:T(8,128)}, u32[]{:S(2)}) copy-start(f32[20,160,160]{2,1,0:T(8,128)} %param.13) | copy-start | bytes 6144004
  8.0 418.9 %reduce-scatter.2.cloned.1.call-start = ((), (), s32[]{:S(2)}) async-start(), calls=%async_computation.3 | async-start | bytes 2359296 | tf_op jit(solution)/shard_map/reduce_scatter | solution.py:172
  10.1 0.8 copy-start.4
  12.0 86.0 %copy-start.6 = (f32[3,32]{1,0:T(4,128)S(1)}, f32[3,32]{1,0:T(4,128)}, u32[]{:S(2)}) copy-start(f32[3,32]{1,0:T(4,128)} %param.16) | copy-start | bytes 1156
  12.0 86.0 %copy-start.8 = (s32[32]{0:T(128)S(1)}, s32[32]{0:T(128)}, u32[]{:S(2)}) copy-start(s32[32]{0:T(128)} %param.17) | copy-start | bytes 388
  109.4 1.9 copy-start.1
  109.4 2.2 copy-start.2
  113.8 6.2 %copy-start.5 = (f32[4,33792]{1,0:T(4,128)S(1)}, f32[4,33792]{1,0:T(4,128)}, u32[]{:S(2)}) copy-start(f32[4,33792]{1,0:T(4,128)} %get-tuple-element.294) | copy-start | bytes 1622020 | tf_op jit(solution)/shard_map/while
  161.1 1.9 copy-start.1
  161.1 2.2 copy-start.2
  165.5 6.2 %copy-start.5 = (f32[4,33792]{1,0:T(4,128)S(1)}, f32[4,33792]{1,0:T(4,128)}, u32[]{:S(2)}) copy-start(f32[4,33792]{1,0:T(4,128)} %get-tuple-element.294) | copy-start | bytes 1622020 | tf_op jit(solution)/shard_map/while
  212.8 1.9 copy-start.1
  212.8 2.2 copy-start.2
  217.2 6.2 %copy-start.5 = (f32[4,33792]{1,0:T(4,128)S(1)}, f32[4,33792]{1,0:T(4,128)}, u32[]{:S(2)}) copy-start(f32[4,33792]{1,0:T(4,128)} %get-tuple-element.294) | copy-start | bytes 1622020 | tf_op jit(solution)/shard_map/while
  264.6 1.9 copy-start.1
  264.6 2.2 copy-start.2
  269.0 6.2 %copy-start.5 = (f32[4,33792]{1,0:T(4,128)S(1)}, f32[4,33792]{1,0:T(4,128)}, u32[]{:S(2)}) copy-start(f32[4,33792]{1,0:T(4,128)} %get-tuple-element.294) | copy-start | bytes 1622020 | tf_op jit(solution)/shard_map/while
  310.2 3.9 copy-start.3
  389.8 25.5 %all-to-all-start = ((f32[8,40,640]{2,1,0:T(8,128)}), f32[8,40,640]{2,1,0:T(8,128)}, u32[]{:S(2)}, u32[]{:S(2)}) async-start(f32[8,40,640]{2,1,0:T(8,128)} %bitcast.207), calls=%async_computation | async-start | bytes 1638400 | tf_op jit(solution)/shard_map/all_to_all | solution.py:74
  396.1 77.9 %all-gather.2.cloned.1.call-start = ((), (), s32[]{:S(2)}) async-start(), calls=%async_computation.2 | async-start | bytes 4096000 | tf_op jit(solution)/shard_map/all_gather | solution.py:83
  397.0 22.9 %copy-start.10 = (f32[2,8,8]{2,1,0:T(8,128)S(1)}, f32[2,8,8]{2,1,0:T(8,128)}, u32[]{:S(2)}) copy-start(f32[2,8,8]{2,1,0:T(8,128)} %param.22) | copy-start | bytes 1540
  399.7 21.8 %copy-start.9 = (s32[32]{0:T(128)S(1)}, s32[32]{0:T(128)}, u32[]{:S(2)}) copy-start(s32[32]{0:T(128)} %param.17) | copy-start | bytes 388
  399.7 21.8 %copy-start.7 = (f32[3,32]{1,0:T(4,128)S(1)}, f32[3,32]{1,0:T(4,128)}, u32[]{:S(2)}) copy-start(f32[3,32]{1,0:T(4,128)} %param.16) | copy-start | bytes 1156
Sparse Core Ops, SparseCore 0:
  305.0 68.7 reduce-scatter.1
Sparse Core Ops, SparseCore 1:
  418.4 29.1 all-gather.1
where the time goes:
time: 489 us; the launch traced here: 485 us
  local copies, waits for them, and re-layouts  197 us (40%)
  matrix products  123 us (25%)
  other arithmetic  79.5 us (16%)
  blocking collectives  41.9 us (9%)
  between operations  15.8 us (3%)
  waiting for transfers between devices  10.9 us (2%)
  loops' own time  10.7 us (2%)
  starting transfers between devices  6.33 us (1%)
    dot_general x4, matrix products, project_block(): jnp.dot(table.reshape(block_rows * 8, waves_here), psi_flat, preferred_el...  96.8 us
    unnamed x19, local copies, waits for them, and re-layouts  88.5 us
    psum x1, blocking collectives, shards(): forces = lax.psum(local_part + nonlocal_full, ('band', 'ga'))  41.9 us
    another operation x4, other arithmetic, project_block(): jnp.stack([radial * jnp.cos(phase)[:, None, :], radial * jnp.sin(phase)[:...  24.7 us
    gather x1, local copies, waits for them, and re-layouts, shards(): picked_rows = jnp.take(columns.T, share_columns, axis=0)  22.7 us
    cos x4, other arithmetic, project_block(): jnp.cos(phase)[:, None, :]  20.9 us
    all_to_all x1, waiting for transfers between devices, shards(): lax.all_to_all(chosen, 'ga', split_axis=0, concat_axis=0, tiled=True)  10.9 us
    another operation x1, loops' own time, shards(): lax.map(one_block, starts)  10.7 us
  transfers between devices with their start and end apart: 3, of which 1 were waited for; matrix products, arithmetic and copies ran while one was open for 23% of the time, Pallas kernels for 0%

commit v1 on v0

--- a/solution.py
+++ b/solution.py
@@ -197,7 +197,7 @@
     nonlocal_full = lax.dynamic_update_slice(
         jnp.zeros((3, atom_count), jnp.float32), nonlocal_part, (start_zero, ga_start)
     )
-    forces = lax.psum(local_part + nonlocal_full, ("band", "ga"))
+    forces = jnp.sum(lax.all_gather(local_part + nonlocal_full, ("band", "ga")), axis=0)
     return (density_sticks, forces)
 
 

time: 489 us -> 518 us (1.059); the launches traced: 485 us -> 508 us
  blocking collectives: 41.9 us -> 64.3 us
    all_gather x0 -> x1, blocking collectives: none -> 64.3 us  [shards(): lax.all_gather(local_part + nonlocal_full, ('band', 'ga'))]
    psum x1 -> x0, blocking collectives: 41.9 us -> none  [shards(): forces = lax.psum(local_part + nonlocal_full, ('band', 'ga'))]
  transfers between devices with their start and end apart: 3 -> 3, of which waited for: 1 -> 1; matrix products, arithmetic and copies ran while one was open for 23% -> 22% of each run, Pallas kernels for 0% -> 0%
where the time goes in v1:
time: 518 us; the launch traced here: 508 us
  local copies, waits for them, and re-layouts  197 us (38%)
  matrix products  123 us (24%)
  other arithmetic  80.1 us (15%)
  blocking collectives  64.3 us (12%)
  between operations  15.8 us (3%)
  waiting for transfers between devices  10.9 us (2%)
  loops' own time  10.7 us (2%)
  starting transfers between devices  6.33 us (1%)
    dot_general x4, matrix products, project_block(): jnp.dot(table.reshape(block_rows * 8, waves_here), psi_flat, preferred_el...  96.8 us
    unnamed x19, local copies, waits for them, and re-layouts  88.5 us
    all_gather x1, blocking collectives, shards(): lax.all_gather(local_part + nonlocal_full, ('band', 'ga'))  64.3 us
    another operation x4, other arithmetic, project_block(): jnp.stack([radial * jnp.cos(phase)[:, None, :], radial * jnp.sin(phase)[:...  24.7 us
    gather x1, local copies, waits for them, and re-layouts, shards(): picked_rows = jnp.take(columns.T, share_columns, axis=0)  22.7 us
    cos x4, other arithmetic, project_block(): jnp.cos(phase)[:, None, :]  20.9 us
    all_to_all x1, waiting for transfers between devices, shards(): lax.all_to_all(chosen, 'ga', split_axis=0, concat_axis=0, tiled=True)  10.9 us
    another operation x1, loops' own time, shards(): lax.map(one_block, starts)  10.7 us
  transfers between devices with their start and end apart: 3, of which 1 were waited for; matrix products, arithmetic and copies ran while one was open for 22% of the time, Pallas kernels for 0%

profile of v1, /device:TPU:12, one launch (start us, length us, event | category | flops | bytes accessed | tf_op | source)
XLA Modules:
  0.0 508.4 jit_solution(16990386369384040606)
XLA Ops:
  8.6 1.4 convert_element_type.119
  12.0 83.8 %copy.56 = bf16[33792,2,256]{0,2,1:T(8,128)(2,1)} copy(bf16[33792,2,256]{2,1,0:T(2,128)(2,1)} %param.18) | data formatting | bytes 69206016 | tf_op args[5]
  95.8 2.2 pad_maximum_fusion.3
  98.0 206.9 %while.12 = (s32[]{:T(128)}, f32[4,64,2048]{2,1,0:T(8,128)}, s32[4]{0:T(128)}, s32[32]{0:T(128)S(1)}, f32[2,8,33792]{2,1,0:T(8,128)}, /*index=5*/f32[3,32]{1,0:T...) while((s32[]{:T(128)}, f32[4,64,2048]{2,1,0:T(8,128)}, ...), condition=%wide.region_3.4_spmd, body=%wide.region_2.3_spmd.sunk | while | flops 17768366080 | bytes 134012464 | solution.py:173
  98.0 1.2 dynamic_slice.49
  101.9 1.9 fusion.115
  103.8 5.2 %fusion.116 = (f32[8,33792]{1,0:T(8,128)}, f32[8,33792]{1,0:T(8,128)}) fusion(f32[33792]{0:T(1024)S(1)} %bitcast.209, f32[8]{0:T(128)S(1)} %get-tuple-element.244, f32[33792]{0:T(1024)S(1)} %bitcast.210, f32[8]{0:T(128)S(1)} %get-tuple-element.246, f32[33792]{0:T(1024)S(1)} %bitcast.208, f32[8]{0:T(128)S(1)} %get-tuple-element.248), kind=kLoop, calls=%fused_computation.14.clone.1 | loop fusion | flops 1622016 | bytes 2568288 | tf_op jit(solution)/shard_map/while/body/eval_jaxpr/cos | solution.py:152
  109.4 1.9 slice_bitcast_fusion.14
  111.6 2.2 bitcast_multiply_fusion.6
  113.8 6.2 %pad_maximum_fusion.8 = f32[64,2,33792]{2,0,1:T(8,128)} fusion(f32[64,1,33792]{2,0,1:T(8,128)S(1)} %get-tuple-element.255, f32[64,1,33792]{2,0,1:T(8,128)S(1)} %get-tuple-element.256), kind=kLoop, calls=%fused_computation.6.clone.1 | loop fusion | flops 4325376 | bytes 34603008 | tf_op jit(solution)/shard_map/while/body/eval_jaxpr/stack | solution.py:151
  120.0 24.2 %fusion.117 = f32[64,4,2,2,256]{4,0,3,2,1:T(8,128)S(1)} fusion(bf16[2,256,33792,1,1]{2,1,0,4,3:T(8,128)(2,1)} %bitcast.203, f32[4,33792]{1,0:T(4,128)S(1)} %copy-done.5, f32[64,2,33792]{2,0,1:T(8,128)} %pad_maximum_fusion.8), kind=kOutput, calls=%fused_computation.3.clone.1 | convolution fusion | flops 17751343104 | bytes 53493760 | tf_op jit(solution)/shard_map/while/body/eval_jaxpr/dot_general | solution.py:155
  145.5 2.3 broadcast_in_dim.34
  147.8 1.9 constant_dynamic-update-slice_fusion.2
  153.6 1.9 fusion.115
  155.5 5.2 %fusion.116 = (f32[8,33792]{1,0:T(8,128)}, f32[8,33792]{1,0:T(8,128)}) fusion(f32[33792]{0:T(1024)S(1)} %bitcast.209, f32[8]{0:T(128)S(1)} %get-tuple-element.244, f32[33792]{0:T(1024)S(1)} %bitcast.210, f32[8]{0:T(128)S(1)} %get-tuple-element.246, f32[33792]{0:T(1024)S(1)} %bitcast.208, f32[8]{0:T(128)S(1)} %get-tuple-element.248), kind=kLoop, calls=%fused_computation.14.clone.1 | loop fusion | flops 1622016 | bytes 2568288 | tf_op jit(solution)/shard_map/while/body/eval_jaxpr/cos | solution.py:152
  161.1 1.9 slice_bitcast_fusion.14
  163.3 2.2 bitcast_multiply_fusion.6
  165.5 6.2 %pad_maximum_fusion.8 = f32[64,2,33792]{2,0,1:T(8,128)} fusion(f32[64,1,33792]{2,0,1:T(8,128)S(1)} %get-tuple-element.255, f32[64,1,33792]{2,0,1:T(8,128)S(1)} %get-tuple-element.256), kind=kLoop, calls=%fused_computation.6.clone.1 | loop fusion | flops 4325376 | bytes 34603008 | tf_op jit(solution)/shard_map/while/body/eval_jaxpr/stack | solution.py:151
  171.7 24.2 %fusion.117 = f32[64,4,2,2,256]{4,0,3,2,1:T(8,128)S(1)} fusion(bf16[2,256,33792,1,1]{2,1,0,4,3:T(8,128)(2,1)} %bitcast.203, f32[4,33792]{1,0:T(4,128)S(1)} %copy-done.5, f32[64,2,33792]{2,0,1:T(8,128)} %pad_maximum_fusion.8), kind=kOutput, calls=%fused_computation.3.clone.1 | convolution fusion | flops 17751343104 | bytes 53493760 | tf_op jit(solution)/shard_map/while/body/eval_jaxpr/dot_general | solution.py:155
  197.2 2.3 broadcast_in_dim.34
  199.5 1.9 constant_dynamic-update-slice_fusion.2
  205.3 1.9 fusion.115
  207.2 5.2 %fusion.116 = (f32[8,33792]{1,0:T(8,128)}, f32[8,33792]{1,0:T(8,128)}) fusion(f32[33792]{0:T(1024)S(1)} %bitcast.209, f32[8]{0:T(128)S(1)} %get-tuple-element.244, f32[33792]{0:T(1024)S(1)} %bitcast.210, f32[8]{0:T(128)S(1)} %get-tuple-element.246, f32[33792]{0:T(1024)S(1)} %bitcast.208, f32[8]{0:T(128)S(1)} %get-tuple-element.248), kind=kLoop, calls=%fused_computation.14.clone.1 | loop fusion | flops 1622016 | bytes 2568288 | tf_op jit(solution)/shard_map/while/body/eval_jaxpr/cos | solution.py:152
  212.8 1.9 slice_bitcast_fusion.14
  215.1 2.2 bitcast_multiply_fusion.6
  217.3 6.2 %pad_maximum_fusion.8 = f32[64,2,33792]{2,0,1:T(8,128)} fusion(f32[64,1,33792]{2,0,1:T(8,128)S(1)} %get-tuple-element.255, f32[64,1,33792]{2,0,1:T(8,128)S(1)} %get-tuple-element.256), kind=kLoop, calls=%fused_computation.6.clone.1 | loop fusion | flops 4325376 | bytes 34603008 | tf_op jit(solution)/shard_map/while/body/eval_jaxpr/stack | solution.py:151
  223.4 24.2 %fusion.117 = f32[64,4,2,2,256]{4,0,3,2,1:T(8,128)S(1)} fusion(bf16[2,256,33792,1,1]{2,1,0,4,3:T(8,128)(2,1)} %bitcast.203, f32[4,33792]{1,0:T(4,128)S(1)} %copy-done.5, f32[64,2,33792]{2,0,1:T(8,128)} %pad_maximum_fusion.8), kind=kOutput, calls=%fused_computation.3.clone.1 | convolution fusion | flops 17751343104 | bytes 53493760 | tf_op jit(solution)/shard_map/while/body/eval_jaxpr/dot_general | solution.py:155
  249.0 2.3 broadcast_in_dim.34
  251.2 1.9 constant_dynamic-update-slice_fusion.2
  257.0 1.9 fusion.115
  258.9 5.2 %fusion.116 = (f32[8,33792]{1,0:T(8,128)}, f32[8,33792]{1,0:T(8,128)}) fusion(f32[33792]{0:T(1024)S(1)} %bitcast.209, f32[8]{0:T(128)S(1)} %get-tuple-element.244, f32[33792]{0:T(1024)S(1)} %bitcast.210, f32[8]{0:T(128)S(1)} %get-tuple-element.246, f32[33792]{0:T(1024)S(1)} %bitcast.208, f32[8]{0:T(128)S(1)} %get-tuple-element.248), kind=kLoop, calls=%fused_computation.14.clone.1 | loop fusion | flops 1622016 | bytes 2568288 | tf_op jit(solution)/shard_map/while/body/eval_jaxpr/cos | solution.py:152
  264.6 1.9 slice_bitcast_fusion.14
  266.8 2.2 bitcast_multiply_fusion.6
  269.0 6.2 %pad_maximum_fusion.8 = f32[64,2,33792]{2,0,1:T(8,128)} fusion(f32[64,1,33792]{2,0,1:T(8,128)S(1)} %get-tuple-element.255, f32[64,1,33792]{2,0,1:T(8,128)S(1)} %get-tuple-element.256), kind=kLoop, calls=%fused_computation.6.clone.1 | loop fusion | flops 4325376 | bytes 34603008 | tf_op jit(solution)/shard_map/while/body/eval_jaxpr/stack | solution.py:151
  275.1 24.2 %fusion.117 = f32[64,4,2,2,256]{4,0,3,2,1:T(8,128)S(1)} fusion(bf16[2,256,33792,1,1]{2,1,0,4,3:T(8,128)(2,1)} %bitcast.203, f32[4,33792]{1,0:T(4,128)S(1)} %copy-done.5, f32[64,2,33792]{2,0,1:T(8,128)} %pad_maximum_fusion.8), kind=kOutput, calls=%fused_computation.3.clone.1 | convolution fusion | flops 17751343104 | bytes 53493760 | tf_op jit(solution)/shard_map/while/body/eval_jaxpr/dot_general | solution.py:155
  300.7 2.3 broadcast_in_dim.34
  302.9 1.9 constant_dynamic-update-slice_fusion.2
  304.9 1.3 fusion.41
  307.7 2.5 fusion.15
  310.3 2.2 fusion.57
  312.5 1.6 convolution_negate_fusion
  314.1 3.5 fusion.55
  317.6 3.6 convolution_add_fusion
  321.2 3.4 copy.50
  324.7 5.5 %reshape.1347 = f32[20,25600]{1,0:T(8,128)} reshape(f32[3200,160]{1,0:T(8,128)} %copy.50) | data formatting | bytes 4096000 | tf_op jit(solution)/shard_map/reshape | solution.py:66
  330.2 6.1 %convolution_subtract_fusion = f32[3200,160]{0,1:T(8,128)} fusion(f32[3200,160]{0,1:T(8,128)} %fusion.55, f32[3200,160]{1,0:T(8,128)} %bitcast.205), kind=kOutput, calls=%fused_computation.31 | convolution fusion | flops 492262400 | bytes 6144000 | tf_op jit(solution)/shard_map/dot_general | solution.py:62
  336.3 3.4 copy.51
  339.7 5.4 %reshape.1348 = f32[20,25600]{1,0:T(8,128)} reshape(f32[3200,160]{1,0:T(8,128)} %copy.51) | data formatting | bytes 4096000 | tf_op jit(solution)/shard_map/reshape | solution.py:66
  345.1 4.7 pad_maximum_fusion.2
  349.9 9.0 %copy.52 = f32[40,25600]{0,1:T(8,128)} copy(f32[40,25600]{1,0:T(8,128)} %pad_maximum_fusion.2) | data formatting | bytes 8192000 | tf_op jit(solution)/shard_map/concatenate | solution.py:65
  358.9 22.7 %gather_fusion = f32[5120,40]{1,0:T(8,128)} fusion(f32[25600,40]{1,0:T(8,128)} %bitcast.201, s32[5120]{0:T(1024)S(1)} %broadcast_clamp_fusion), kind=kCustom, calls=%fused_computation | custom fusion | bytes 1658880 | tf_op jit(solution)/shard_map/jit(_take)/gather | solution.py:72
  381.7 5.3 %broadcast_select_fusion = f32[5120,40]{1,0:T(8,128)} fusion(f32[5120,40]{1,0:T(8,128)} %gather_fusion, pred[5120]{0:T(1024)(128)(4,1)S(1)} %compare_and_fusion), kind=kLoop, calls=%fused_computation.41 | loop fusion | flops 204800 | bytes 1643520 | tf_op jit(solution)/shard_map/jit(_take)/select_n | solution.py:72
  386.9 2.8 copy.53
  389.8 6.3 %all-to-all-start = ((f32[8,40,640]{2,1,0:T(8,128)}), f32[8,40,640]{2,1,0:T(8,128)}, u32[]{:S(2)}, u32[]{:S(2)}) async-start(f32[8,40,640]{2,1,0:T(8,128)} %bitcast.212), calls=%async_computation | async-start | bytes 1638400 | tf_op jit(solution)/shard_map/all_to_all | solution.py:74
  397.9 1.7 stack.25
  400.8 1.8 stack.27
  402.6 1.8 copy.49
  404.4 10.9 %all-to-all-done = f32[8,40,640]{2,1,0:T(8,128)} async-done(((f32[8,40,640]{2,1,0:T(8,128)}), f32[8,40,640]{2,1,0:T(8,128)}, u32[]{:S(2)}, u32[]{:S(2)}) %all-to-all-start) | async-done | bytes 819232 | tf_op jit(solution)/shard_map/all_to_all | solution.py:74
  415.2 3.0 fusion.27
  423.8 2.4 fusion.20
  426.9 1.2 reshape.1354
  430.8 1.4 add.268
  432.1 64.3 %all_gather.14 = f32[32,3,32]{2,1,0:T(4,128)S(1)} all-gather(f32[1,3,32]{2,1,0:T(4,128)} %add.268), channel_id=1, replica_groups=mesh['band'=4,'ga'=8] {'band','ga'}, dimensions={0}, use_global_device_ids=true | all-gather | bytes 12672 | tf_op jit(solution)/shard_map/all_gather | solution.py:200
  497.1 3.9 copy.109
  (135 shorter events, 28.6 us)
Async XLA Ops:
  8.0 299.7 %copy-start = (f32[20,160,160]{2,1,0:T(8,128)S(1)}, f32[20,160,160]{2,1,0:T(8,128)}, u32[]{:S(2)}) copy-start(f32[20,160,160]{2,1,0:T(8,128)} %param.13) | copy-start | bytes 6144004
  8.0 418.9 %reduce-scatter.2.cloned.1.call-start = ((), (), s32[]{:S(2)}) async-start(), calls=%async_computation.3 | async-start | bytes 2359296 | tf_op jit(solution)/shard_map/reduce_scatter | solution.py:172
  10.1 0.8 copy-start.4
  12.0 86.0 %copy-start.6 = (f32[3,32]{1,0:T(4,128)S(1)}, f32[3,32]{1,0:T(4,128)}, u32[]{:S(2)}) copy-start(f32[3,32]{1,0:T(4,128)} %param.16) | copy-start | bytes 1156
  12.0 86.0 %copy-start.8 = (s32[32]{0:T(128)S(1)}, s32[32]{0:T(128)}, u32[]{:S(2)}) copy-start(s32[32]{0:T(128)} %param.17) | copy-start | bytes 388
  109.4 1.9 copy-start.1
  109.4 2.2 copy-start.2
  113.8 6.2 %copy-start.5 = (f32[4,33792]{1,0:T(4,128)S(1)}, f32[4,33792]{1,0:T(4,128)}, u32[]{:S(2)}) copy-start(f32[4,33792]{1,0:T(4,128)} %get-tuple-element.294) | copy-start | bytes 1622020 | tf_op jit(solution)/shard_map/while
  161.1 1.9 copy-start.1
  161.1 2.2 copy-start.2
  165.5 6.2 %copy-start.5 = (f32[4,33792]{1,0:T(4,128)S(1)}, f32[4,33792]{1,0:T(4,128)}, u32[]{:S(2)}) copy-start(f32[4,33792]{1,0:T(4,128)} %get-tuple-element.294) | copy-start | bytes 1622020 | tf_op jit(solution)/shard_map/while
  212.8 1.9 copy-start.1
  212.8 2.2 copy-start.2
  217.2 6.2 %copy-start.5 = (f32[4,33792]{1,0:T(4,128)S(1)}, f32[4,33792]{1,0:T(4,128)}, u32[]{:S(2)}) copy-start(f32[4,33792]{1,0:T(4,128)} %get-tuple-element.294) | copy-start | bytes 1622020 | tf_op jit(solution)/shard_map/while
  264.6 1.9 copy-start.1
  264.6 2.2 copy-start.2
  269.0 6.2 %copy-start.5 = (f32[4,33792]{1,0:T(4,128)S(1)}, f32[4,33792]{1,0:T(4,128)}, u32[]{:S(2)}) copy-start(f32[4,33792]{1,0:T(4,128)} %get-tuple-element.294) | copy-start | bytes 1622020 | tf_op jit(solution)/shard_map/while
  310.2 3.9 copy-start.3
  389.8 25.5 %all-to-all-start = ((f32[8,40,640]{2,1,0:T(8,128)}), f32[8,40,640]{2,1,0:T(8,128)}, u32[]{:S(2)}, u32[]{:S(2)}) async-start(f32[8,40,640]{2,1,0:T(8,128)} %bitcast.212), calls=%async_computation | async-start | bytes 1638400 | tf_op jit(solution)/shard_map/all_to_all | solution.py:74
  396.1 101.0 %all-gather.2.cloned.1.call-start = ((), (), s32[]{:S(2)}) async-start(), calls=%async_computation.2 | async-start | bytes 4096000 | tf_op jit(solution)/shard_map/all_gather | solution.py:83
  397.0 22.9 %copy-start.10 = (f32[2,8,8]{2,1,0:T(8,128)S(1)}, f32[2,8,8]{2,1,0:T(8,128)}, u32[]{:S(2)}) copy-start(f32[2,8,8]{2,1,0:T(8,128)} %param.22) | copy-start | bytes 1540
  399.7 21.8 %copy-start.9 = (s32[32]{0:T(128)S(1)}, s32[32]{0:T(128)}, u32[]{:S(2)}) copy-start(s32[32]{0:T(128)} %param.17) | copy-start | bytes 388
  399.7 21.8 %copy-start.7 = (f32[3,32]{1,0:T(4,128)S(1)}, f32[3,32]{1,0:T(4,128)}, u32[]{:S(2)}) copy-start(f32[3,32]{1,0:T(4,128)} %param.16) | copy-start | bytes 1156
Sparse Core Ops, SparseCore 0:
  305.0 68.7 reduce-scatter.1
Sparse Core Ops, SparseCore 1:
  418.4 28.5 all-gather.1
